TPU v7x, 128 devices: a whole 4x4x4 slice. The times are simulated.
128 devices in a mesh: wide: 32 (over y, x, core), narrow: 4 (over z).
Axes of the slice: x: 4, y: 4, z: 4, core: 2. Of those that a mesh axis runs over, the one named last changes fastest.
Arguments:
- slab: float32 [96, 512, 8192], P('narrow', 'wide'), may hold values from -24 to 24, as said below
- start: float32 [512, 64], replicated, may hold values from -6 to 6
Outputs:
- core: float32 [96, 64, 8192], P('narrow', None, 'wide')
- factor: float32 [512, 64], replicated
Inputs may be any that keep to these rules, and one draw needn't show every extreme that they name: The slab is a planted sum of 64 separable terms plus noise.
All inputs are finite; a program needn't handle non-finite values.
Results may differ from a plain program's by a relative error of at most 0.0003.
Values sent between devices are 32-bit elements; how exact they have to be, the bound alone decides.
A program may use at most 256 MiB of HBM per device.

v0:
```python
import jax
import jax.numpy as jnp
from jax import lax
from jax.sharding import PartitionSpec as P

ITERS = 2


def orthonormal(matrix):
    product = jnp.dot(matrix.T, matrix, precision=lax.Precision.HIGHEST)
    lower = jnp.linalg.cholesky(product)
    return lax.linalg.triangular_solve(lower, matrix, left_side=False, lower=True, transpose_a=True)


def block_gram(block):
    return jnp.einsum("nix,njx->ij", block, block, precision=lax.Precision.HIGHEST)


def on_device(slab, start):
    fibres = lax.all_to_all(slab, "wide", split_axis=2, concat_axis=1, tiled=True)
    local_gram = block_gram(fibres)
    basis = orthonormal(start)
    gram = lax.psum(local_gram, ("wide", "narrow"))
    for step in range(ITERS):
        basis = orthonormal(jnp.dot(gram, basis, precision=lax.Precision.HIGHEST))
    core = jnp.einsum("ik,sif->skf", basis, fibres, precision=lax.Precision.HIGHEST)
    return (core, basis)


def solution(mesh):
    placed = (P("narrow", "wide", None), P())
    return jax.shard_map(
        on_device,
        mesh=mesh,
        in_specs=placed,
        out_specs=(P("narrow", None, "wide"), P()),
        check_vma=False,
    )
```

profile of v0, /device:TPU:1, one launch (start us, length us, event | category | flops | bytes accessed | tf_op | source)
XLA Modules:
  0.0 642.3 jit_solution(10626874872593620060)
XLA Ops:
  7.2 33.5 %copy.13 = f32[24,16,8192]{0,1,2:T(8,128)} copy(f32[24,16,8192]{2,1,0:T(8,128)} %param.5) | data formatting | bytes 25165824 | tf_op args[0]
  40.7 57.8 %reshape.27 = f32[32,1,98304]{2,1,0:T(1,128)} reshape(f32[8192,16,24]{2,1,0:T(8,128)} %bitcast.44) | data formatting | bytes 25165824
  98.5 8.6 %all-to-all-start = ((f32[32,1,98304]{2,1,0:T(1,128)}), f32[32,1,98304]{2,1,0:T(1,128)}, u32[]{:S(2)}, u32[]{:S(2)}) async-start(f32[32,1,98304]{2,1,0:T(1,128)} %reshape.27), calls=%async_computation | async-start | bytes 25165824 | tf_op jit(solution)/shard_map/all_to_all | solution.py:20
  107.6 5.8 cholesky.59
  113.5 145.2 %all-to-all-done = f32[32,1,98304]{2,1,0:T(1,128)} async-done(((f32[32,1,98304]{2,1,0:T(1,128)}), f32[32,1,98304]{2,1,0:T(1,128)}, u32[]{:S(2)}, u32[]{:S(2)}) %all-to-all-start) | async-done | bytes 12582944 | tf_op jit(solution)/shard_map/all_to_all | solution.py:20
  259.2 36.7 %reduce.4 = f32[32,98304]{1,0:T(8,128)} reduce(f32[32,1,98304]{2,1,0:T(1,128)} %all-to-all-done, f32[]{:T(128)} %broadcast.37), dimensions={1}, to_apply=%all_to_all.13.reduce_sub_computation | reduce | bytes 25165828 | tf_op jit(solution)/shard_map/all_to_all | solution.py:20
  296.0 78.6 %reshape.28 = f32[8192,16,24]{2,1,0:T(8,128)} reshape(f32[32,98304]{1,0:T(8,128)} %reduce.4) | data formatting | bytes 25165824
  374.6 40.1 %copy.14 = f32[24,16,32,256]{3,1,2,0:T(8,128)} copy(f32[24,16,32,256]{0,1,3,2:T(8,128)} %bitcast) | data formatting | bytes 25165824 | tf_op jit(solution)/shard_map/all_to_all | solution.py:20
  414.7 24.7 %convolution_bitcast_fusion.1 = f32[512,512]{1,0:T(8,128)} fusion(f32[24,512,256]{2,1,0:T(8,128)} %bitcast.62), kind=kOutput, calls=%fused_computation.1 | convolution fusion | flops 19327352832 | bytes 13631488 | tf_op jit(solution)/shard_map/nix,njx->ij/dot_general | solution.py:16
  439.5 0.6 compare_reduce_fusion.2
  440.1 0.7 fusion.1
  440.8 4.9 custom-call.7
  446.0 147.3 %all-reduce.2.cloned.1.call-done = f32[512,512]{1,0:T(8,128)} async-done(((f32[512,512]{1,0:T(8,128)}), f32[512,512]{1,0:T(8,128)}) %all-reduce.2.cloned.1.call-update) | async-done | bytes 1048592 | tf_op jit(solution)/shard_map/psum | solution.py:23
  593.3 2.4 fusion.16
  596.1 5.8 cholesky.70
  601.9 0.6 compare_reduce_fusion.1
  602.6 0.7 fusion.2
  603.3 4.9 custom-call.8
  608.5 2.4 fusion.18
  611.2 5.8 cholesky.81
  617.1 0.6 compare_reduce_fusion
  617.7 0.7 fusion.3
  618.4 4.9 custom-call.9
  623.6 11.8 %convolution_bitcast_fusion = f32[24,64,256]{2,1,0:T(8,128)} fusion(f32[24,512,256]{2,1,0:T(8,128)} %bitcast.63, f32[64,512]{1,0:T(8,128)S(1)} %fusion.4), kind=kOutput, calls=%fused_computation | convolution fusion | flops 2415919104 | bytes 14286848 | tf_op jit(solution)/shard_map/ik,sif->skf/dot_general | solution.py:26
  (22 shorter events, 2.7 us)
Async XLA Ops:
  7.2 100.1 %copy-start = (f32[512,64]{0,1:T(8,128)S(1)}, f32[512,64]{0,1:T(8,128)}, u32[]{:S(2)}) copy-start(f32[512,64]{0,1:T(8,128)} %param.6) | copy-start | bytes 393220
  98.5 160.2 %all-to-all-start = ((f32[32,1,98304]{2,1,0:T(1,128)}), f32[32,1,98304]{2,1,0:T(1,128)}, u32[]{:S(2)}, u32[]{:S(2)}) async-start(f32[32,1,98304]{2,1,0:T(1,128)} %reshape.27), calls=%async_computation | async-start | bytes 25165824 | tf_op jit(solution)/shard_map/all_to_all | solution.py:20
  107.2 486.2 %all-reduce.2.cloned.1.call-start = ((), (), s32[]{:S(2)}) async-start(), calls=%async_computation.1 | async-start | bytes 2097152 | tf_op jit(solution)/shard_map/psum | solution.py:23
  623.6 11.8 %copy-start.1 = (f32[64,512]{1,0:T(8,128)}, f32[64,512]{1,0:T(8,128)S(1)}, u32[]{:S(2)}) copy-start(f32[64,512]{1,0:T(8,128)S(1)} %fusion.4) | copy-start | bytes 393220
Sparse Core Ops, SparseCore 0:
  439.6 153.6 all-reduce.1
where the time goes:
time: 645 us; the launch traced here: 642 us
  waiting for transfers between devices  293 us (45%)
  local copies, waits for them, and re-layouts  211 us (33%)
  other arithmetic  73 us (11%)
  matrix products  43 us (7%)
  between operations  14.2 us (2%)
  starting transfers between devices  8.68 us (1%)
    unnamed x7, local copies, waits for them, and re-layouts  170 us
    psum x1, waiting for transfers between devices, on_device(): gram = lax.psum(local_gram, ('wide', 'narrow'))  147 us
    all_to_all x1, waiting for transfers between devices, on_device(): lax.all_to_all(slab, 'wide', split_axis=2, concat_axis=1, tiled=True)  145 us
    all_to_all x2, local copies, waits for them, and re-layouts, on_device(): lax.all_to_all(slab, 'wide', split_axis=2, concat_axis=1, tiled=True)  40.6 us
    all_to_all x1, other arithmetic, on_device(): lax.all_to_all(slab, 'wide', split_axis=2, concat_axis=1, tiled=True)  36.7 us
    dot_general x1, matrix products, block_gram(): jnp.einsum('nix,njx->ij', block, block, precision=lax.Precision.HIGHEST)  24.7 us
    another operation x9, other arithmetic, orthonormal(): lower = jnp.linalg.cholesky(product)  19.6 us
    another operation x6, other arithmetic, orthonormal(): lax.linalg.triangular_solve(lower, matrix, left_side=False, lower=True, t...  16.6 us
  transfers between devices with their start and end apart: 2, of which 2 were waited for; matrix products, arithmetic and copies ran while one was open for 2% of the time, Pallas kernels for 0%

commit v1 on v0

--- a/solution.py
+++ b/solution.py
@@ -17,7 +17,10 @@
 
 
 def on_device(slab, start):
-    fibres = lax.all_to_all(slab, "wide", split_axis=2, concat_axis=1, tiled=True)
+    fibres = jnp.concatenate(
+        lax.all_to_all(jnp.stack(jnp.split(slab, lax.axis_size("wide"), axis=2)), "wide", 0, 0),
+        axis=1,
+    )
     local_gram = block_gram(fibres)
     basis = orthonormal(start)
     gram = lax.psum(local_gram, ("wide", "narrow"))

time: 645 us -> 465 us (0.72)
  local copies, waits for them, and re-layouts: 211 us -> 68.5 us
  other arithmetic: 73 us -> 36.2 us
    unnamed x7 -> x35, local copies, waits for them, and re-layouts: 170 us -> 55.1 us
    all_to_all x2 -> x0, local copies, waits for them, and re-layouts: 40.6 us -> none  [on_device(): lax.all_to_all(slab, 'wide', split_axis=2, concat_axis=1, tiled=True)]
    all_to_all x1 -> x0, other arithmetic: 36.7 us -> none  [on_device(): lax.all_to_all(slab, 'wide', split_axis=2, concat_axis=1, tiled=True)]
    reshape x0 -> x1, local copies, waits for them, and re-layouts: none -> 11.4 us  [on_device(): jnp.concatenate(lax.all_to_all(jnp.stack(jnp.split(slab, lax.axis_size('w...]
  transfers between devices with their start and end apart: 2 -> 2, of which waited for: 2 -> 2; matrix products, arithmetic and copies ran while one was open for 2% -> 3% of each run, Pallas kernels for 0% -> 0%
where the time goes in v1:
time: 465 us; the launch traced here: 464 us
  waiting for transfers between devices  293 us (63%)
  local copies, waits for them, and re-layouts  68.5 us (15%)
  matrix products  43.6 us (9%)
  other arithmetic  36.2 us (8%)
  between operations  14.2 us (3%)
  starting transfers between devices  8.68 us (2%)
    psum x1, waiting for transfers between devices, on_device(): gram = lax.psum(local_gram, ('wide', 'narrow'))  147 us
    all_to_all x1, waiting for transfers between devices, on_device(): lax.all_to_all(jnp.stack(jnp.split(slab, lax.axis_size('wide'), axis=2)),...  145 us
    unnamed x35, local copies, waits for them, and re-layouts  55.1 us
    dot_general x1, matrix products, block_gram(): jnp.einsum('nix,njx->ij', block, block, precision=lax.Precision.HIGHEST)  24.7 us
    another operation x9, other arithmetic, orthonormal(): lower = jnp.linalg.cholesky(product)  19.6 us
    another operation x6, other arithmetic, orthonormal(): lax.linalg.triangular_solve(lower, matrix, left_side=False, lower=True, t...  16.6 us
    dot_general x1, matrix products, on_device(): jnp.einsum('ik,sif->skf', basis, fibres, precision=lax.Precision.HIGHEST)  12.4 us
    reshape x1, local copies, waits for them, and re-layouts, on_device(): jnp.concatenate(lax.all_to_all(jnp.stack(jnp.split(slab, lax.axis_size('w...  11.4 us
  transfers between devices with their start and end apart: 2, of which 2 were waited for; matrix products, arithmetic and copies ran while one was open for 3% of the time, Pallas kernels for 0%

profile of v1, /device:TPU:1, one launch (start us, length us, event | category | flops | bytes accessed | tf_op | source)
XLA Modules:
  0.0 463.8 jit_solution(6301869120156648215)
XLA Ops:
  7.2 1.8 bitcast_dynamic-update-slice_fusion.31
  12.5 1.8 bitcast_dynamic-update-slice_fusion.28
  16.1 1.8 bitcast_dynamic-update-slice_fusion.26
  28.4 1.8 bitcast_dynamic-update-slice_fusion.19
  32.0 1.8 bitcast_dynamic-update-slice_fusion.17
  35.6 1.8 bitcast_dynamic-update-slice_fusion.15
  44.4 1.8 bitcast_dynamic-update-slice_fusion.10
  48.0 1.8 bitcast_dynamic-update-slice_fusion.8
  51.6 1.8 bitcast_dynamic-update-slice_fusion.6
  55.2 1.8 bitcast_dynamic-update-slice_fusion.4
  64.0 8.6 %all-to-all-start = ((f32[32,24,16,256]{3,2,1,0:T(8,128)}), f32[32,24,16,256]{3,2,1,0:T(8,128)}, u32[]{:S(2)}, u32[]{:S(2)}) async-start(f32[32,24,16,256]{3,2,1,0:T(8,128)} %bitcast_dynamic-update-slice_fusion), calls=%async_computation | async-start | bytes 25165824 | tf_op jit(solution)/shard_map/all_to_all | solution.py:21
  73.1 5.8 %cholesky.59 = f32[64,64]{1,0:T(8,128)S(1)} custom-call(f32[64,64]{1,0:T(8,128)S(1)} %fusion.10), custom_call_target="Cholesky" | custom-call | tf_op jit(solution)/shard_map/jit(cholesky)/cholesky | solution.py:11
  79.0 145.2 %all-to-all-done = f32[32,24,16,256]{3,2,1,0:T(8,128)} async-done(((f32[32,24,16,256]{3,2,1,0:T(8,128)}), f32[32,24,16,256]{3,2,1,0:T(8,128)}, u32[]{:S(2)}, u32[]{:S(2)}) %all-to-all-start) | async-done | bytes 12582944 | tf_op jit(solution)/shard_map/all_to_all | solution.py:21
  224.2 11.4 %copy.4 = f32[24,32,16,256]{3,2,1,0:T(8,128)} copy(f32[24,32,16,256]{3,2,0,1:T(8,128)} %bitcast.32) | data formatting | bytes 25165824 | tf_op jit(solution)/shard_map/reshape | solution.py:20
  235.6 24.7 %convolution_bitcast_fusion.1 = f32[512,512]{1,0:T(8,128)} fusion(f32[24,512,256]{2,1,0:T(8,128)} %bitcast.122), kind=kOutput, calls=%fused_computation.1 | convolution fusion | flops 19327352832 | bytes 13631488 | tf_op jit(solution)/shard_map/nix,njx->ij/dot_general | solution.py:16
  261.7 4.9 %custom-call.7 = f32[1,64,64]{1,2,0:T(8,128)S(1)} custom-call(f32[1,64,64]{2,1,0:T(8,128)S(1)} %fusion.1), custom_call_target="InvertDiagBlocksLowerTriangular" | custom-call | tf_op jit(solution)/shard_map/triangular_solve/custom-call.0 | solution.py:12
  266.9 147.3 %all-reduce.2.cloned.1.call-done = f32[512,512]{1,0:T(8,128)} async-done(((f32[512,512]{1,0:T(8,128)}), f32[512,512]{1,0:T(8,128)}) %all-reduce.2.cloned.1.call-update) | async-done | bytes 1048592 | tf_op jit(solution)/shard_map/psum | solution.py:26
  414.2 2.4 fusion.16
  417.0 5.8 %cholesky.70 = f32[64,64]{1,0:T(8,128)S(1)} custom-call(f32[64,64]{1,0:T(8,128)S(1)} %fusion.8), custom_call_target="Cholesky" | custom-call | tf_op jit(solution)/shard_map/jit(cholesky)/cholesky | solution.py:11
  424.1 4.9 %custom-call.8 = f32[1,64,64]{1,2,0:T(8,128)S(1)} custom-call(f32[1,64,64]{2,1,0:T(8,128)S(1)} %fusion.2), custom_call_target="InvertDiagBlocksLowerTriangular" | custom-call | tf_op jit(solution)/shard_map/triangular_solve/custom-call.0 | solution.py:12
  429.4 2.4 fusion.18
  432.1 5.8 %cholesky.81 = f32[64,64]{1,0:T(8,128)S(1)} custom-call(f32[64,64]{1,0:T(8,128)S(1)} %fusion.6), custom_call_target="Cholesky" | custom-call | tf_op jit(solution)/shard_map/jit(cholesky)/cholesky | solution.py:11
  439.3 4.9 %custom-call.9 = f32[1,64,64]{1,2,0:T(8,128)S(1)} custom-call(f32[1,64,64]{2,1,0:T(8,128)S(1)} %fusion.3), custom_call_target="InvertDiagBlocksLowerTriangular" | custom-call | tf_op jit(solution)/shard_map/triangular_solve/custom-call.0 | solution.py:12
  444.5 12.4 %convolution_bitcast_fusion = f32[24,64,256]{2,1,0:T(8,128)} fusion(f32[24,512,256]{2,1,0:T(8,128)} %bitcast.123, f32[64,512]{1,0:T(8,128)S(1)} %fusion.4), kind=kOutput, calls=%fused_computation | convolution fusion | flops 2415919104 | bytes 14286848 | tf_op jit(solution)/shard_map/ik,sif->skf/dot_general | solution.py:29
  (49 shorter events, 45.0 us)
Async XLA Ops:
  7.2 65.6 %copy-start = (f32[512,64]{0,1:T(8,128)S(1)}, f32[512,64]{0,1:T(8,128)}, u32[]{:S(2)}) copy-start(f32[512,64]{0,1:T(8,128)} %param.6) | copy-start | bytes 393220
  64.0 160.2 %all-to-all-start = ((f32[32,24,16,256]{3,2,1,0:T(8,128)}), f32[32,24,16,256]{3,2,1,0:T(8,128)}, u32[]{:S(2)}, u32[]{:S(2)}) async-start(f32[32,24,16,256]{3,2,1,0:T(8,128)} %bitcast_dynamic-update-slice_fusion), calls=%async_computation | async-start | bytes 25165824 | tf_op jit(solution)/shard_map/all_to_all | solution.py:21
  72.7 341.5 %all-reduce.2.cloned.1.call-start = ((), (), s32[]{:S(2)}) async-start(), calls=%async_computation.1 | async-start | bytes 2097152 | tf_op jit(solution)/shard_map/psum | solution.py:26
  444.5 12.4 %copy-start.1 = (f32[64,512]{1,0:T(8,128)}, f32[64,512]{1,0:T(8,128)S(1)}, u32[]{:S(2)}) copy-start(f32[64,512]{1,0:T(8,128)S(1)} %fusion.4) | copy-start | bytes 393220
Sparse Core Ops, SparseCore 0:
  260.5 153.6 all-reduce.1
